TPU v7x, 512 devices: a whole 4x4x16 slice. The times are simulated.
512 devices in a mesh: ctx: 64 (over y, z), exp: 8 (over x, core).
Axes of the slice: x: 4, y: 4, z: 16, core: 2. Of those that a mesh axis runs over, the one named last changes fastest.
Arguments:
- queries: bfloat16 [8192, 4096], P('ctx', 'exp'), may hold values from -24 to 24
- key_rows: bfloat16 [8192, 1024], P('ctx', 'exp'), may hold values from -24 to 24
- mixer_input: bfloat16 [8192, 8192], P('ctx', 'exp'), may hold values from -32 to 32
- gate_input: bfloat16 [8192, 8192], P('ctx', 'exp'), may hold values from -6 to 6
- write_proj: bfloat16 [8192, 128], P('ctx'), may hold values from -0.5 to 0.5
- read_proj: bfloat16 [8192, 128], P('ctx'), may hold values from -0.5 to 0.5
- step_size: float32 [8192, 128], P('ctx', 'exp'), may hold values from 0.5 to 2
- log_decay: float32 [8192, 128], P('ctx', 'exp'), may hold values from -1.7 to 0
- skip_gain: float32 [128], P('exp'), may hold values from 0.5 to 2
- norm_gain: float32 [8192], P('exp'), may hold values from 0.1 to 1.9
- value_weight: bfloat16 [8192, 1024], P('exp'), may hold values from -0.09375 to 0.09375
Outputs:
- attention_out: bfloat16 [8192, 4096], P('ctx', 'exp')
- mixer_out: bfloat16 [8192, 8192], P('ctx', 'exp')
All inputs are finite; a program needn't handle non-finite values.
Results may differ from a plain program's by a relative error of at most 0.018.
Values may be sent and summed in bfloat16 or wider, within the bound.
A program may use at most 64 MiB of HBM per device.

v0:
```python
import jax
import jax.numpy as jnp
from jax import lax
from jax.sharding import PartitionSpec as P

QUERY_HEADS = 32
KEY_HEADS = 8
HEAD_DIM = 128
MIXER_HEADS = 128
MIXER_CHANNELS = 64
STATE_SIZE = 128
BLOCK_LEN = 128


rope_base = 10000.0
rope_stretch = 4.0
norm_eps = 1e-05
floor_score = -1e30


def entering(x, axis, join, neutral):
    place = lax.axis_index(axis)
    gathered = jax.tree.map(
        lambda a, kind: lax.all_gather(a.astype(kind), axis), x, (jnp.bfloat16, jnp.bfloat16)
    )
    state = jax.tree.map(lambda a, e: jnp.zeros_like(a) + jnp.asarray(e, a.dtype), x, neutral)

    def one(lap, state):
        return join(
            state,
            jax.tree.map(
                lambda a, own: lax.dynamic_index_in_dim(a, lap, 0, False).astype(own.dtype),
                gathered,
                x,
            ),
        )

    return lax.fori_loop(0, place, one, state)


def rotate(vectors, positions, head_width):
    halfway = head_width // 2
    frequency = rope_base ** (-(2.0 * jnp.arange(halfway, dtype=jnp.float32)) / head_width)
    angles = (positions.astype(jnp.float32) / rope_stretch)[:, None] * frequency[None, :]
    cosine = jnp.cos(angles)[:, None, :]
    sine_part = jnp.sin(angles)[:, None, :]
    front_half = vectors[..., :halfway].astype(jnp.float32)
    back_half = vectors[..., halfway:].astype(jnp.float32)
    turned = jnp.concatenate(
        [front_half * cosine - back_half * sine_part, back_half * cosine + front_half * sine_part],
        axis=-1,
    )
    return turned.astype(jnp.bfloat16)


def attend_update(
    running, query_group, query_pos, key_block, value_block, key_pos, group_low, group_high
):
    running_max, running_sum, running_out = running
    scores = jnp.einsum(
        "cgtd,scd->cgts", query_group, key_block, preferred_element_type=jnp.float32
    ) * HEAD_DIM ** (-0.5)
    allowed = key_pos[None, :] <= query_pos[:, None]
    masked = jnp.where(allowed, scores, floor_score)
    new_max = jnp.maximum(running_max, jnp.max(masked, axis=-1))
    weights = jnp.where(allowed, jnp.exp(masked - new_max[..., None]), 0.0)
    factor = jnp.exp(running_max - new_max)
    new_sum = running_sum * factor + jnp.sum(weights, axis=-1)
    update = jnp.einsum(
        "cgts,scd->cgtd",
        weights.astype(jnp.bfloat16),
        value_block,
        preferred_element_type=jnp.float32,
    )
    new_out = running_out * factor[..., None] + update
    return (
        running_max.at[:, :, group_low:group_high].set(new_max),
        running_sum.at[:, :, group_low:group_high].set(new_sum),
        running_out.at[:, :, group_low:group_high].set(new_out),
    )


def attention(queries, key_rows, value_rows):
    row_count = queries.shape[0]
    kv_local = key_rows.shape[1] // HEAD_DIM
    group_size = QUERY_HEADS // KEY_HEADS
    shard_index = lax.axis_index("ctx")
    local_pos = jnp.arange(row_count, dtype=jnp.int32)
    groups = ((0, row_count),)
    query_pos = shard_index * row_count + local_pos
    turned_q = rotate(
        queries.reshape(row_count, kv_local * group_size, HEAD_DIM), query_pos, HEAD_DIM
    )
    query_mat = jnp.transpose(
        turned_q.reshape(row_count, kv_local, group_size, HEAD_DIM), (1, 2, 0, 3)
    )
    turned_k = rotate(key_rows.reshape(row_count, kv_local, HEAD_DIM), query_pos, HEAD_DIM)
    value_mat = value_rows.reshape(row_count, kv_local, HEAD_DIM)
    initial = (
        jnp.full((kv_local, group_size, row_count), floor_score, jnp.float32),
        jnp.zeros((kv_local, group_size, row_count), jnp.float32),
        jnp.zeros((kv_local, group_size, row_count, HEAD_DIM), jnp.float32),
    )
    piece_keys = lax.all_gather(turned_k, "ctx", axis=0, tiled=True)
    piece_values = lax.all_gather(value_mat, "ctx", axis=0, tiled=True)
    piece_rows = piece_keys.shape[0]
    piece_pos = jnp.arange(piece_rows, dtype=jnp.int32)

    def key_step(step_index, current):
        offset = step_index * row_count
        block_keys = lax.dynamic_slice_in_dim(piece_keys, offset, row_count, 0)
        block_values = lax.dynamic_slice_in_dim(piece_values, offset, row_count, 0)
        block_pos = lax.dynamic_slice_in_dim(piece_pos, offset, row_count, 0)
        group_low, group_high = groups[0]
        group_pos = query_pos

        def group_update(state_in, group_low=group_low, group_high=group_high, group_pos=group_pos):
            return attend_update(
                state_in,
                query_mat,
                group_pos,
                block_keys,
                block_values,
                block_pos,
                group_low,
                group_high,
            )

        def unchanged(state_in):
            return state_in

        needed = jnp.min(block_pos) <= jnp.max(group_pos)
        current = lax.cond(needed, group_update, unchanged, current)
        return current

    result = lax.fori_loop(0, piece_rows // row_count, key_step, initial)
    running_max, running_sum, running_out = result
    merged = running_out / running_sum[..., None]
    finished = (
        jnp.transpose(merged, (2, 0, 1, 3))
        .reshape(row_count, kv_local * group_size * HEAD_DIM)
        .astype(jnp.bfloat16)
    )
    return finished


def chain_join(earlier, later):
    return (earlier[0] + later[0], jnp.exp(later[0])[:, None, None] * earlier[1] + later[1])


def mixer_block(
    mixer_input, gate_input, write_proj, read_proj, step_size, log_decay, skip_gain, norm_gain
):
    row_count = mixer_input.shape[0]
    head_count = step_size.shape[1]
    block_count = row_count // BLOCK_LEN
    shaped_x = mixer_input.reshape(block_count, BLOCK_LEN, head_count, MIXER_CHANNELS)
    causal = jnp.arange(BLOCK_LEN)[:, None] >= jnp.arange(BLOCK_LEN)[None, :]
    agg_state = jnp.zeros((head_count, MIXER_CHANNELS, STATE_SIZE), jnp.float32)
    block_x = shaped_x[0]
    block_read = read_proj
    cumul = jnp.cumsum(log_decay, axis=0)
    gram = jnp.einsum("tn,sn->ts", block_read, write_proj, preferred_element_type=jnp.float32)
    cumul_heads = cumul.T
    spread = cumul_heads[:, :, None] - cumul_heads[:, None, :]
    decay = jnp.where(causal[None], jnp.exp(jnp.where(causal[None], spread, 0.0)), 0.0)
    mixing = (decay * gram[None] * step_size.T[:, None, :]).astype(jnp.bfloat16)
    intra = jnp.einsum("hts,shp->thp", mixing, block_x, preferred_element_type=jnp.float32)
    ending = cumul[-1]
    weighted = (
        block_x.astype(jnp.float32) * (step_size * jnp.exp(ending[None, :] - cumul))[:, :, None]
    ).astype(jnp.bfloat16)
    local_state = jnp.einsum(
        "shp,sn->hpn", weighted, write_proj, preferred_element_type=jnp.float32
    )
    agg_state = jnp.exp(ending)[:, None, None] * agg_state + local_state
    agg_decay = ending
    saved = (intra, cumul, ending, local_state, block_read, block_x)
    incoming = entering(
        (agg_decay, agg_state),
        "ctx",
        chain_join,
        (
            jnp.zeros((head_count,), jnp.float32),
            jnp.zeros((head_count, MIXER_CHANNELS, STATE_SIZE), jnp.float32),
        ),
    )
    carried = incoming[1]
    intra, cumul, ending, local_state, block_read, block_x = saved
    inter = (
        jnp.einsum(
            "tn,hpn->thp", block_read.astype(jnp.float32), carried, precision=lax.Precision.HIGHEST
        )
        * jnp.exp(cumul)[:, :, None]
    )
    pieces_out = intra + inter + skip_gain[None, :, None] * block_x.astype(jnp.float32)
    gate_full = gate_input.reshape(row_count, head_count, MIXER_CHANNELS).astype(jnp.float32)
    gated = pieces_out * jax.nn.silu(gate_full)
    partial_square = jnp.sum(gated * gated, axis=(1, 2))
    total_square = lax.psum(partial_square, "exp")
    mean_square = total_square / (MIXER_HEADS * MIXER_CHANNELS)
    normed = (
        gated
        * lax.rsqrt(mean_square + norm_eps)[:, None, None]
        * norm_gain.reshape(head_count, MIXER_CHANNELS)
    )
    return normed.reshape(row_count, head_count * MIXER_CHANNELS).astype(jnp.bfloat16)


def on_device(
    queries,
    key_rows,
    mixer_input,
    gate_input,
    write_proj,
    read_proj,
    step_size,
    log_decay,
    skip_gain,
    norm_gain,
    value_weight,
):
    mixer_out = mixer_block(
        mixer_input, gate_input, write_proj, read_proj, step_size, log_decay, skip_gain, norm_gain
    )
    value_terms = jnp.dot(mixer_out, value_weight, preferred_element_type=jnp.float32)
    value_rows = lax.psum_scatter(
        value_terms.astype(jnp.bfloat16), "exp", scatter_dimension=1, tiled=True
    )
    attention_out = attention(queries, key_rows, value_rows)
    return (attention_out, mixer_out)


def solution(mesh):
    return jax.shard_map(
        on_device,
        mesh=mesh,
        in_specs=(
            P("ctx", "exp"),
            P("ctx", "exp"),
            P("ctx", "exp"),
            P("ctx", "exp"),
            P("ctx", None),
            P("ctx", None),
            P("ctx", "exp"),
            P("ctx", "exp"),
            P("exp"),
            P("exp"),
            P("exp", None),
        ),
        out_specs=(P("ctx", "exp"), P("ctx", "exp")),
        check_vma=False,
    )
```

profile of v0, /device:TPU:504, one launch (start us, length us, event | category | flops | bytes accessed | tf_op | source)
XLA Modules:
  0.0 883.1 jit_solution(17325050694433945698)
XLA Ops:
  12.2 70.4 %all-gather.2 = bf16[64,1,16]{2,1,0:T(2,128)(2,1)S(1)} all-gather(bf16[1,1,16]{2,1,0:T(2,128)(2,1)S(1)} %convert_bitcast_fusion), channel_id=1, replica_groups=mesh['ctx'=64,'exp'=8] {'ctx'}, dimensions={0}, use_global_device_ids=true | all-gather | bytes 2080 | tf_op jit(solution)/shard_map/all_gather | solution.py:24
  84.7 114.7 %all-gather.9.cloned.1.call-done = bf16[1024,64,128]{2,1,0:T(8,128)(2,1)} async-done(((bf16[16,64,128]{2,1,0:T(8,128)(2,1)}), bf16[1024,64,128]{2,1,0:T(8,128)(2,1)}) %all-gather.9.cloned.1.call-update) | async-done | bytes 16777232 | tf_op jit(solution)/shard_map/all_gather | solution.py:24
  199.5 73.2 %while.37 = (s32[]{:T(128)}, f32[16,64,128]{2,1,0:T(8,128)S(1)}, s32[]{:T(128)}, bf16[64,16]{1,0:T(8,128)(2,1)S(1)}, bf16[64,16,64,128]{3,2,1,0:T(8,128)(2,1)}, /*index=5*/s32[]{:T(128)}, s32[]{:T(128)}, s32[]{:T(128)}) while((s32[]{:T(128)}, f32[16,64,128]{2,1,0:T(8,128)S(1)}, s32[]{:T(128)}, bf16[64,16]{1,0:T(8,128)(2,1)S(1)}, ...), condition=%wide.region_2.3_spmd, body=%wide.region_1.2_spmd.sunk | while | flops 393237 | bytes 1311007 | solution.py:38
  272.6 2.3 multiply_reduce_fusion
  275.0 13.8 %psum.7 = f32[128]{0:T(128)S(1)} all-reduce(f32[128]{0:T(128)S(1)} %get-tuple-element.521), channel_id=1, replica_groups=mesh['ctx'=64,'exp'=8] {'exp'}, use_global_device_ids=true, to_apply=%region_4.5 | all-reduce | flops 128 | bytes 1024 | tf_op jit(solution)/shard_map/psum | solution.py:200
  292.4 29.7 %reduce-scatter.4.cloned.1.call-done = bf16[128,128]{1,0:T(8,128)(2,1)} async-done(((bf16[1024,128]{1,0:T(8,128)(2,1)}), bf16[128,128]{1,0:T(8,128)(2,1)}) %reduce-scatter.4.cloned.1.call-update) | async-done | bytes 32784
  324.8 132.9 %all-gather.7.cloned.1.call-done = bf16[8192,1,128]{0,2,1:T(8,128)(2,1)} async-done(((bf16[128,1,128]{0,2,1:T(8,128)(2,1)}), bf16[8192,1,128]{0,2,1:T(8,128)(2,1)}) %all-gather.7.cloned.1.call-update) | async-done | bytes 2097168 | tf_op jit(solution)/shard_map/all_gather | solution.py:104
  457.7 4.1 copy.67
  462.6 134.0 %all-gather.11.cloned.1.call-done = bf16[8192,128]{1,0:T(8,128)(2,1)} async-done(((bf16[128,128]{1,0:T(8,128)(2,1)}), bf16[8192,128]{1,0:T(8,128)(2,1)}) %all-gather.11.cloned.1.call-update) | async-done | bytes 2097168 | tf_op jit(solution)/shard_map/all_gather | solution.py:105
  596.7 278.9 %while.38 = (s32[]{:T(128)}, f32[1,4,128]{2,1,0:T(4,128)S(1)}, f32[1,4,128]{2,1,0:T(4,128)S(1)}, f32[1,4,128,128]{3,2,1,0:T(8,128)S(1)}, s32[8192]{0:T(1024)S(1)...) while((s32[]{:T(128)}, f32[1,4,128]{2,1,0:T(4,128)S(1)}, ...), condition=%wide.region_13.14_spmd.clone, body=%wide.region_7.0_spmd.clone.sunk | while | flops 34293512 | bytes 1610581 | solution.py:136
  598.8 2.2 conditional.3
  603.2 2.2 conditional.3
  607.5 2.2 conditional.3
  611.9 2.2 conditional.3
  616.2 2.2 conditional.3
  620.6 2.2 conditional.3
  624.9 2.2 conditional.3
  629.3 2.2 conditional.3
  633.7 2.2 conditional.3
  638.0 2.2 conditional.3
  642.4 2.2 conditional.3
  646.7 2.2 conditional.3
  655.4 2.2 conditional.3
  659.8 2.2 conditional.3
  664.2 2.2 conditional.3
  672.9 2.2 conditional.3
  677.2 2.2 conditional.3
  681.6 2.2 conditional.3
  690.3 2.2 conditional.3
  694.7 2.2 conditional.3
  699.0 2.2 conditional.3
  707.7 2.2 conditional.3
  712.1 2.2 conditional.3
  716.5 2.2 conditional.3
  720.8 2.2 conditional.3
  725.2 2.2 conditional.3
  729.5 2.2 conditional.3
  733.9 2.2 conditional.3
  738.2 2.2 conditional.3
  742.6 2.2 conditional.3
  747.0 2.2 conditional.3
  751.3 2.2 conditional.3
  755.7 2.2 conditional.3
  760.0 2.2 conditional.3
  764.4 2.2 conditional.3
  768.8 2.2 conditional.3
  773.1 2.2 conditional.3
  777.5 2.2 conditional.3
  786.2 2.2 conditional.3
  790.5 2.2 conditional.3
  794.9 2.2 conditional.3
  803.6 2.2 conditional.3
  808.0 2.2 conditional.3
  812.3 2.2 conditional.3
  821.0 2.2 conditional.3
  825.4 2.2 conditional.3
  829.8 2.2 conditional.3
  838.5 2.2 conditional.3
  842.8 2.2 conditional.3
  847.2 2.2 conditional.3
  855.9 2.2 conditional.3
  860.3 2.2 conditional.3
  864.6 2.2 conditional.3
  873.3 2.2 conditional.3
  (845 shorter events, 297.7 us)
Async XLA Ops:
  7.2 282.9 %copy-start = (bf16[1024,1024]{1,0:T(8,128)(2,1)S(1)}, bf16[1024,1024]{1,0:T(8,128)(2,1)}, u32[]{:S(2)}) copy-start(bf16[1024,1024]{1,0:T(8,128)(2,1)} %param.39) | copy-start | bytes 6291460
  7.2 76.1 %copy-start.6 = (f32[128,16]{0,1:T(8,128)S(1)}, f32[128,16]{0,1:T(8,128)}, u32[]{:S(2)}) copy-start(f32[128,16]{0,1:T(8,128)} %param.35) | copy-start | bytes 24580
  7.2 76.0 %copy-start.3 = (bf16[128,128]{1,0:T(8,128)(2,1)S(1)}, bf16[128,128]{1,0:T(8,128)(2,1)}, u32[]{:S(2)}) copy-start(bf16[128,128]{1,0:T(8,128)(2,1)} %param.33) | copy-start | bytes 98308
  7.2 75.6 %copy-start.1 = (bf16[128,1024]{1,0:T(8,128)(2,1)S(1)}, bf16[128,1024]{1,0:T(8,128)(2,1)}, u32[]{:S(2)}) copy-start(bf16[128,1024]{1,0:T(8,128)(2,1)} %param.32) | copy-start | bytes 786436
  7.2 75.7 %copy-start.7 = (f32[1024]{0:T(1024)S(1)}, f32[1024]{0:T(1024)}, u32[]{:S(2)}) copy-start(f32[1024]{0:T(1024)} %param.38) | copy-start | bytes 12292
  7.2 75.8 %copy-start.4 = (bf16[128,128]{1,0:T(8,128)(2,1)S(1)}, bf16[128,128]{1,0:T(8,128)(2,1)}, u32[]{:S(2)}) copy-start(bf16[128,128]{1,0:T(8,128)(2,1)} %param.30) | copy-start | bytes 98308
  7.2 76.0 %copy-start.5 = (bf16[128,128]{1,0:T(8,128)(2,1)S(1)}, bf16[128,128]{1,0:T(8,128)(2,1)}, u32[]{:S(2)}) copy-start(bf16[128,128]{1,0:T(8,128)(2,1)} %param.34) | copy-start | bytes 98308
  7.2 192.2 %all-gather.9.cloned.1.call-start = ((), (), s32[]{:S(2)}) async-start(), calls=%async_computation.2 | async-start | bytes 17039360 | tf_op jit(solution)/shard_map/all_gather | solution.py:24
  12.2 309.9 %reduce-scatter.4.cloned.1.call-start = ((), (), s32[]{:S(2)}) async-start(), calls=%async_computation.4 | async-start | bytes 294912
  199.5 73.2 %copy-start.8 = (f32[16]{0:T(128)S(1)}, f32[16]{0:T(128)}, u32[]{:S(2)}) copy-start(f32[16]{0:T(128)} %param.37) | copy-start | bytes 196
  288.8 35.5 %copy-start.2 = (bf16[128,512]{1,0:T(8,128)(2,1)S(1)}, bf16[128,512]{1,0:T(8,128)(2,1)}, u32[]{:S(2)}) copy-start(bf16[128,512]{1,0:T(8,128)(2,1)} %param.29) | copy-start | bytes 393220
  291.4 166.3 %all-gather.7.cloned.1.call-start = ((), (), s32[]{:S(2)}) async-start(), calls=%async_computation.1 | async-start | bytes 2129920 | tf_op jit(solution)/shard_map/all_gather | solution.py:104
  292.4 304.3 %all-gather.11.cloned.1.call-start = ((), (), s32[]{:S(2)}) async-start(), calls=%async_computation.3 | async-start | bytes 2129920 | tf_op jit(solution)/shard_map/all_gather | solution.py:105
Sparse Core Ops, SparseCore 0:
  12.3 187.0 all-gather.8
  291.6 30.4 reduce-scatter.3
  325.6 132.0 all-gather.6
  460.5 136.0 all-gather.10
where the time goes:
time: 895 us; the launch traced here: 883 us
  waiting for transfers between devices  411 us (46%)
  other arithmetic  135 us (15%)
  matrix products  134 us (15%)
  loops' own time  91.8 us (10%)
  blocking collectives  84.2 us (9%)
  between operations  14 us (2%)
  local copies, waits for them, and re-layouts  12.1 us (1%)
    all_gather x1, waiting for transfers between devices, attention(): piece_values = lax.all_gather(value_mat, 'ctx', axis=0, tiled=True)  134 us
    all_gather x1, waiting for transfers between devices, attention(): piece_keys = lax.all_gather(turned_k, 'ctx', axis=0, tiled=True)  133 us
    all_gather x1, waiting for transfers between devices, entering(): lax.all_gather(a.astype(kind), axis)  115 us
    another operation x1, loops' own time, attention(): result = lax.fori_loop(0, piece_rows // row_count, key_step, initial)  86 us
    all_gather x1, blocking collectives, entering(): lax.all_gather(a.astype(kind), axis)  70.4 us
    add x63, other arithmetic, chain_join(): jnp.exp(later[0])[:, None, None] * earlier[1] + later[1]  70 us
    dot_general x64, matrix products, attend_update(): jnp.einsum('cgts,scd->cgtd', weights.astype(jnp.bfloat16), value_block, p...  66.4 us
    dot_general x64, matrix products, attend_update(): jnp.einsum('cgtd,scd->cgts', query_group, key_block, preferred_element_ty...  61.9 us
  transfers between devices with their start and end apart: 4, of which 4 were waited for; matrix products, arithmetic and copies ran while one was open for 1% of the time, Pallas kernels for 0%

commit v1 on v0

v1 whole, which is shorter than its diff:
```python
import functools

import jax
import jax.numpy as jnp
import numpy as np
from jax import lax
from jax.experimental import pallas as pl
from jax.experimental.pallas import tpu as pltpu
from jax.sharding import PartitionSpec as P

HEAD_DIM = 128
MIXER_CHANNELS = 64
TOKENS = 128
LANES = 128
ROWS_Y = 4
ROPE_BASE = 10000.0
ROPE_STRETCH = 4.0
NORM_EPS = 1e-05
LOWEST = -1e30
MESH = pl.DeviceIdType.MESH
F32 = jnp.float32
BF16 = jnp.bfloat16
HIGHEST = lax.Precision.HIGHEST
EXP2_SCALE = float(HEAD_DIM**-0.5 * np.log2(np.e))


def dot(a, b, dims=((1,), (0,)), precision=None):
    return lax.dot_general(
        a, b, (dims, ((), ())), precision=precision, preferred_element_type=F32
    )


def kernel(
    ctx_size,
    exp_size,
    q_ref,
    k_ref,
    x_ref,
    gate_ref,
    write_ref,
    read_ref,
    step_ref,
    decay_ref,
    skip_ref,
    gain_ref,
    freq_ref,
    weight_ref,
    attn_ref,
    mixer_ref,
    local_state,
    state_in,
    state_out,
    state_back,
    ends_own,
    ends_all,
    pad_a,
    pad_b,
    decay_rows,
    gated_ref,
    scaled_ref,
    terms_ref,
    terms_in,
    square_own,
    square_in,
    turned_q,
    key_all,
    value_all,
    score_ref,
    prob_ref,
    top_ref,
    sum_ref,
    out_ref,
    a2a_send,
    a2a_recv,
    exp_send,
    exp_recv,
    ring_send,
    key_recv,
    value_recv,
):
    z_size = ctx_size // ROWS_Y
    half = z_size // 2
    heads = step_ref.shape[1]
    pairs = heads // 2
    groups = q_ref.shape[1] // HEAD_DIM
    state_rows = heads * MIXER_CHANNELS // ctx_size
    me = lax.axis_index("ctx")
    col = lax.axis_index("exp")
    my_y = lax.div(me, z_size)
    my_z = lax.rem(me, z_size)

    barrier = pltpu.get_barrier_semaphore()

    def greet_ctx(i, c):
        pl.semaphore_signal(
            barrier, inc=1, device_id={"ctx": lax.rem(me + i, ctx_size)}, device_id_type=MESH
        )
        return c

    lax.fori_loop(1, ctx_size, greet_ctx, 0)

    def greet_exp(i, c):
        pl.semaphore_signal(
            barrier, inc=1, device_id={"exp": lax.rem(col + i, exp_size)}, device_id_type=MESH
        )
        return c

    lax.fori_loop(1, exp_size, greet_exp, 0)

    row = lax.broadcasted_iota(jnp.int32, (TOKENS, LANES), 0)
    lane = lax.broadcasted_iota(jnp.int32, (TOKENS, LANES), 1)
    first = lane < MIXER_CHANNELS
    causal = row >= lane

    def spread(columns, j):
        return jnp.where(first, columns[:, 2 * j : 2 * j + 1], columns[:, 2 * j + 1 : 2 * j + 2])

    position = (me * TOKENS + row).astype(F32)
    angle = (position * (1.0 / ROPE_STRETCH)) * freq_ref[...]
    cosine = jnp.cos(angle)
    sine = jnp.sin(angle)
    sine = jnp.where(first, -sine, sine)

    def turn(v):
        v = v.astype(F32)
        return (v * cosine + pltpu.roll(v, HEAD_DIM // 2, 1) * sine).astype(BF16)

    key_all[me] = turn(k_ref[...])

    tri = jnp.where(causal, 1.0, 0.0).astype(F32)
    cumul = dot(tri, decay_ref[...], precision=HIGHEST)
    ending = cumul[TOKENS - 1 : TOKENS, :]
    ends_own[...] = jnp.zeros_like(ends_own)
    ends_own[0, :, 0:heads] = ending
    ends_all[me] = ends_own[0]
    carry_weight = step_ref[...] * jnp.exp(ending - cumul)
    for j in range(pairs):
        weighted = x_ref[:, j * LANES : (j + 1) * LANES].astype(F32) * spread(carry_weight, j)
        turned = jnp.transpose(weighted).astype(BF16)
        local = dot(turned, write_ref[...]).astype(BF16)
        per = LANES // state_rows
        local_state[j * per : (j + 1) * per] = local.reshape(per, state_rows, LANES)
    state_in[me] = local_state[me]

    pl.semaphore_wait(barrier, ctx_size + exp_size - 2)

    def exchange(source, target, by_peer):
        def one(i, c):
            part, turn_y = lax.div(i, ROWS_Y), lax.rem(lax.rem(i, ROWS_Y) + 1, ROWS_Y)
            odd = lax.rem(part, 2)
            shift = half + (1 - 2 * odd) * lax.div(part + 1, 2)
            peer = lax.rem(my_y + turn_y, ROWS_Y) * z_size + lax.rem(my_z + shift, z_size)
            pltpu.make_async_remote_copy(
                src_ref=source.at[peer if by_peer else 0],
                dst_ref=target.at[me],
                send_sem=a2a_send.at[sem_at[0]],
                recv_sem=a2a_recv.at[sem_at[0]],
                device_id={"ctx": peer},
                device_id_type=MESH,
            ).start()
            return c

        lax.fori_loop(0, ctx_size - 1, one, 0)

    def exchange_wait(target):
        whole = target.at[pl.ds(0, ctx_size - 1)]
        done = pltpu.make_async_remote_copy(
            src_ref=whole,
            dst_ref=whole,
            send_sem=a2a_send.at[sem_at[0]],
            recv_sem=a2a_recv.at[sem_at[0]],
            device_id={"ctx": me},
            device_id_type=MESH,
        )
        done.wait_send()
        done.wait_recv()

    block_b = jnp.where(my_y == 3, 1, 0)
    up_row = jnp.where(my_y == 1, 2, 3)
    right = my_y * z_size + lax.rem(my_z + 1, z_size)
    left = my_y * z_size + lax.rem(my_z + z_size - 1, z_size)

    def push(buffer, recv, index, peer, sem):
        pltpu.make_async_remote_copy(
            src_ref=buffer.at[index],
            dst_ref=buffer.at[index],
            send_sem=sem,
            recv_sem=recv.at[index],
            device_id={"ctx": peer},
            device_id_type=MESH,
        ).start()

    def arrived(buffer, recv, index, sem):
        pltpu.make_async_remote_copy(
            src_ref=buffer.at[index],
            dst_ref=buffer.at[index],
            send_sem=sem,
            recv_sem=recv.at[index],
            device_id={"ctx": me},
            device_id_type=MESH,
        ).wait_recv()

    def ring_open(buffer, recv, sem):
        push(buffer, recv, me, right, sem)
        if half > 1:
            push(buffer, recv, me, left, sem)

        @pl.when(my_y == 0)
        def _():
            push(buffer, recv, me, z_size + my_z, sem)
            push(buffer, recv, me, 2 * z_size + my_z, sem)

        @pl.when(my_y == 1)
        def _():
            push(buffer, recv, me, 3 * z_size + my_z, sem)

        @pl.when(my_y < 3)
        def _():
            push(buffer, recv, me, up_row * z_size + my_z, sem)

    def ring_steps(low, high, buffer, recv, sem, compute):
        def step(s, c):
            @pl.when((s >= 1) & (s <= half))
            def _():
                at = lax.rem(my_z - s + z_size, z_size)
                own = my_y * z_size + at
                arrived(buffer, recv, own, sem)

                @pl.when(s < half)
                def _():
                    push(buffer, recv, own, right, sem)

                @pl.when(my_y < 3)
                def _():
                    push(buffer, recv, own, up_row * z_size + my_z, sem)

            @pl.when((s >= 1) & (s < half))
            def _():
                at = lax.rem(my_z + s, z_size)
                own = my_y * z_size + at
                arrived(buffer, recv, own, sem)

                @pl.when(s < half - 1)
                def _():
                    push(buffer, recv, own, left, sem)

                @pl.when(my_y < 3)
                def _():
                    push(buffer, recv, own, up_row * z_size + my_z, sem)

            @pl.when((my_y > 0) & (s <= half))
            def _():
                at = lax.rem(my_z - s + z_size, z_size)
                other = block_b * z_size + at
                arrived(buffer, recv, other, sem)

                @pl.when(s < half)
                def _():
                    push(buffer, recv, other, right, sem)

                if half > 1:

                    @pl.when(s == 0)
                    def _():
                        push(buffer, recv, other, left, sem)

            @pl.when((my_y > 0) & (s >= 1) & (s < half))
            def _():
                at = lax.rem(my_z + s, z_size)
                other = block_b * z_size + at
                arrived(buffer, recv, other, sem)

                @pl.when(s < half - 1)
                def _():
                    push(buffer, recv, other, left, sem)

            def visit(j, c):
                side, row_y = lax.div(j, ROWS_Y), lax.rem(j, ROWS_Y)
                relayed = (row_y != my_y) & (row_y != block_b) & (row_y < my_y)
                back = s - jnp.where(relayed, 1, 0)
                span = jnp.where(side == 0, back, z_size - back)
                index = row_y * z_size + lax.rem(my_z - span + 2 * z_size, z_size)
                low_ok = back >= side
                high_ok = back <= half - side
                valid = low_ok & high_ok & (row_y <= my_y)

                @pl.when(valid & relayed)
                def _():
                    arrived(buffer, recv, index, sem)

                @pl.when(valid & (index < me))
                def _():
                    compute(index)

                return c

            lax.fori_loop(0, 2 * ROWS_Y, visit, 0)
            return c

        lax.fori_loop(low, high, step, 0)

    ring_total = half + 2

    def ring_close(buffer, sem):
        ring = z_size - 1
        for y, count in enumerate((ring + 2 + z_size, 2 * ring + 1 + z_size, 2 * ring + z_size, 2 * ring)):

            @pl.when(my_y == y)
            def _():
                for part in range(0, count, ctx_size):
                    size = min(ctx_size, count - part)
                    whole = buffer.at[pl.ds(0, size)]
                    pltpu.make_async_remote_copy(
                        src_ref=whole,
                        dst_ref=whole,
                        send_sem=sem,
                        recv_sem=sem,
                        device_id={"ctx": me},
                        device_id_type=MESH,
                    ).wait_send()

    sem_at = [0]
    ring_open(key_all, key_recv, ring_send.at[0])
    exchange(ends_own, ends_all, False)
    sem_at[0] = 1
    exchange(local_state, state_in, True)

    for g in range(groups):
        turned_q[g] = turn(q_ref[:, g * HEAD_DIM : (g + 1) * HEAD_DIM])

    def score(g, index):
        return dot(turned_q[g], key_all[index], ((1,), (1,)))

    for g in range(groups):
        own_score = jnp.where(causal, score(g, me), LOWEST)
        score_ref[me, g] = own_score
        top_ref[g] = own_score

    def key_block(index):
        for g in range(groups):
            s = score(g, index)
            score_ref[index, g] = s
            top_ref[g] = jnp.maximum(top_ref[g], s)

    pad_a[...] = jnp.zeros_like(pad_a)
    pad_b[...] = jnp.zeros_like(pad_b)
    pad_a[:, 0:heads] = cumul
    pad_b[:, 0:heads] = step_ref[...]
    cumul_t = jnp.transpose(pad_a[...])
    step_t = jnp.transpose(pad_b[...])
    gram = dot(read_ref[...], write_ref[...], ((1,), (1,)))
    for j in range(pairs):
        x_pair = x_ref[:, j * LANES : (j + 1) * LANES]
        total = None
        for part in range(2):
            h = 2 * j + part
            exponent = jnp.where(causal, cumul[:, h : h + 1] - cumul_t[h : h + 1, :], LOWEST)
            mixing = (jnp.exp(exponent) * gram * step_t[h : h + 1, :]).astype(BF16)
            keep = first if part == 0 else jnp.logical_not(first)
            term = dot(mixing, jnp.where(keep, x_pair, jnp.zeros_like(x_pair)))
            total = term if total is None else total + term
        skip = jnp.where(
            first[0:1], skip_ref[0:1, 2 * j : 2 * j + 1], skip_ref[0:1, 2 * j + 1 : 2 * j + 2]
        )
        gated_ref[:, j * LANES : (j + 1) * LANES] = total + skip * x_pair.astype(F32)

    split_a, split_b = min(SPLIT[0], ring_total), min(SPLIT[1], ring_total)
    ring_steps(0, split_a, key_all, key_recv, ring_send.at[0], key_block)

    sem_at[0] = 0
    exchange_wait(ends_all)
    head = lax.div(me * state_rows, MIXER_CHANNELS)
    chosen = jnp.where(row == head, 1.0, 0.0).astype(F32)
    decay_rows[...] = jnp.exp(
        dot(ends_all[...].reshape(ctx_size, LANES), chosen, precision=HIGHEST)
    )
    sem_at[0] = 1
    exchange_wait(state_in)

    def scan(b, state):
        state_out[b] = state.astype(BF16)
        return state * decay_rows[pl.ds(b, 1), :] + state_in[b].astype(F32)

    lax.fori_loop(0, ctx_size, scan, jnp.zeros((state_rows, LANES), F32), unroll=8)
    state_back[me] = state_out[me]
    sem_at[0] = 2
    exchange(state_out, state_back, True)

    ring_steps(split_a, split_b, key_all, key_recv, ring_send.at[0], key_block)

    exchange_wait(state_back)
    growth = jnp.exp(cumul)
    squares = jnp.zeros((TOKENS, LANES), F32)
    per = LANES // state_rows
    for j in range(pairs):
        at = slice(j * LANES, (j + 1) * LANES)
        state = state_back[j * per : (j + 1) * per].reshape(LANES, LANES)
        inter = dot(read_ref[...], state, ((1,), (1,))) * spread(growth, j)
        gate = gate_ref[:, at].astype(F32)
        gated = (gated_ref[:, at] + inter) * (gate / (1.0 + jnp.exp(-gate)))
        squares = squares + gated * gated
        scaled = gated * gain_ref[0:1, at]
        gated_ref[:, at] = scaled
        scaled_ref[:, at] = scaled.astype(BF16)
    ones = jnp.ones((8, LANES), F32)
    square_own[0] = dot(ones, squares, ((1,), (1,)), precision=HIGHEST)
    for e in range(exp_size):
        terms = dot(scaled_ref[...], weight_ref[:, e * LANES : (e + 1) * LANES])
        terms_ref[e] = terms.astype(BF16)
    terms_in[col] = terms_ref[col]
    square_in[col] = square_own[0]

    def scatter(i, c):
        peer = lax.rem(col + i, exp_size)
        pltpu.make_async_remote_copy(
            src_ref=square_own.at[0],
            dst_ref=square_in.at[col],
            send_sem=exp_send.at[0],
            recv_sem=exp_recv.at[0],
            device_id={"exp": peer},
            device_id_type=MESH,
        ).start()
        pltpu.make_async_remote_copy(
            src_ref=terms_ref.at[peer],
            dst_ref=terms_in.at[col],
            send_sem=exp_send.at[1],
            recv_sem=exp_recv.at[1],
            device_id={"exp": peer},
            device_id_type=MESH,
        ).start()
        return c

    lax.fori_loop(1, exp_size, scatter, 0)

    ring_steps(split_b, ring_total, key_all, key_recv, ring_send.at[0], key_block)
    ring_close(key_all, ring_send.at[0])

    for g in range(groups):
        top_ref[g] = jnp.broadcast_to(jnp.max(top_ref[g], axis=1, keepdims=True), (TOKENS, LANES))
        sum_ref[g] = jnp.zeros((TOKENS, LANES), F32)
        out_ref[g] = jnp.zeros((TOKENS, LANES), F32)

    def weigh(b, c):
        for g in range(groups):
            p = jnp.exp2((score_ref[b, g] - top_ref[g]) * EXP2_SCALE)
            sum_ref[g] += p
            prob_ref[b, g] = p.astype(BF16)
        return c

    lax.fori_loop(0, me + 1, weigh, 0)

    for slot, target in ((0, square_in), (1, terms_in)):
        whole = target.at[pl.ds(0, exp_size - 1)]
        done = pltpu.make_async_remote_copy(
            src_ref=whole,
            dst_ref=whole,
            send_sem=exp_send.at[slot],
            recv_sem=exp_recv.at[slot],
            device_id={"exp": col},
            device_id_type=MESH,
        )
        done.wait_send()
        done.wait_recv()
    square_row = square_in[0]
    for e in range(1, exp_size):
        square_row = square_row + square_in[e]
    square = jnp.transpose(jnp.broadcast_to(square_row[0:1, :], (TOKENS, LANES)))
    factor = lax.rsqrt(square * (1.0 / (exp_size * heads * MIXER_CHANNELS)) + NORM_EPS)
    value = terms_in[0].astype(F32)
    for e in range(1, exp_size):
        value = value + terms_in[e].astype(F32)
    value_all[me] = (value * factor).astype(BF16)
    ring_open(value_all, value_recv, ring_send.at[1])

    for j in range(pairs):
        at = slice(j * LANES, (j + 1) * LANES)
        mixer_ref[:, at] = (gated_ref[:, at] * factor).astype(BF16)

    def value_block(index):
        for g in range(groups):
            out_ref[g] += dot(prob_ref[index, g], value_all[index])

    value_block(me)
    ring_steps(0, ring_total, value_all, value_recv, ring_send.at[1], value_block)
    for g in range(groups):
        total = jnp.sum(sum_ref[g], axis=1, keepdims=True)
        attn_ref[:, g * HEAD_DIM : (g + 1) * HEAD_DIM] = (out_ref[g] / total).astype(BF16)
    ring_close(value_all, ring_send.at[1])


SPLIT = (4, 8)


def solution(mesh):
    ctx_size, exp_size = mesh.shape["ctx"], mesh.shape["exp"]

    def on_device(
        queries,
        key_rows,
        mixer_input,
        gate_input,
        write_proj,
        read_proj,
        step_size,
        log_decay,
        skip_gain,
        norm_gain,
        value_weight,
    ):
        heads = step_size.shape[1]
        channels = heads * MIXER_CHANNELS
        groups = queries.shape[1] // HEAD_DIM
        state_rows = channels // ctx_size
        frequency = ROPE_BASE ** (-(2.0 * np.arange(HEAD_DIM // 2)) / HEAD_DIM)
        frequency = jnp.asarray(np.tile(frequency, 2)[None, :], F32)
        vmem = functools.partial(pl.BlockSpec, memory_space=pltpu.VMEM)
        tile = (TOKENS, LANES)
        return pl.pallas_call(
            functools.partial(kernel, ctx_size, exp_size),
            out_shape=(
                jax.ShapeDtypeStruct(queries.shape, BF16),
                jax.ShapeDtypeStruct(mixer_input.shape, BF16),
            ),
            in_specs=[vmem()] * 12,
            out_specs=(vmem(), vmem()),
            scratch_shapes=[
                pltpu.VMEM((ctx_size, state_rows, LANES), BF16),
                pltpu.VMEM((ctx_size, state_rows, LANES), BF16),
                pltpu.VMEM((ctx_size, state_rows, LANES), BF16),
                pltpu.VMEM((ctx_size, state_rows, LANES), BF16),
                pltpu.VMEM((1, 1, LANES), F32),
                pltpu.VMEM((ctx_size, 1, LANES), F32),
                pltpu.VMEM(tile, F32),
                pltpu.VMEM(tile, F32),
                pltpu.VMEM((ctx_size, LANES), F32),
                pltpu.VMEM((TOKENS, channels), F32),
                pltpu.VMEM((TOKENS, channels), BF16),
                pltpu.VMEM((exp_size,) + tile, BF16),
                pltpu.VMEM((exp_size,) + tile, BF16),
                pltpu.VMEM((1, 8, LANES), F32),
                pltpu.VMEM((exp_size, 8, LANES), F32),
                pltpu.VMEM((groups,) + tile, BF16),
                pltpu.VMEM((ctx_size,) + tile, BF16),
                pltpu.VMEM((ctx_size,) + tile, BF16),
                pltpu.VMEM((ctx_size, groups) + tile, F32),
                pltpu.VMEM((ctx_size, groups) + tile, BF16),
                pltpu.VMEM((groups,) + tile, F32),
                pltpu.VMEM((groups,) + tile, F32),
                pltpu.VMEM((groups,) + tile, F32),
                pltpu.SemaphoreType.DMA((3,)),
                pltpu.SemaphoreType.DMA((3,)),
                pltpu.SemaphoreType.DMA((2,)),
                pltpu.SemaphoreType.DMA((2,)),
                pltpu.SemaphoreType.DMA((2,)),
                pltpu.SemaphoreType.DMA((ctx_size,)),
                pltpu.SemaphoreType.DMA((ctx_size,)),
            ],
            compiler_params=pltpu.CompilerParams(
                collective_id=0, has_side_effects=True, vmem_limit_bytes=56 * 1024 * 1024
            ),
        )(
            queries,
            key_rows,
            mixer_input,
            gate_input,
            write_proj,
            read_proj,
            step_size,
            log_decay,
            skip_gain.reshape(1, heads),
            norm_gain.reshape(1, channels),
            frequency,
            value_weight,
        )

    return jax.shard_map(
        on_device,
        mesh=mesh,
        in_specs=(
            P("ctx", "exp"),
            P("ctx", "exp"),
            P("ctx", "exp"),
            P("ctx", "exp"),
            P("ctx", None),
            P("ctx", None),
            P("ctx", "exp"),
            P("ctx", "exp"),
            P("exp"),
            P("exp"),
            P("exp", None),
        ),
        out_specs=(P("ctx", "exp"), P("ctx", "exp")),
        check_vma=False,
    )
```

time: 895 us -> 110 us (0.12)
  the two profiles are of different devices: /device:TPU:504 before, /device:TPU:24 now
where the time goes in v1:
time: 110 us
  Pallas kernels  103 us (94%)
  local copies, waits for them, and re-layouts  6.09 us (6%)
    pallas_call x1, Pallas kernels, on_device(): pl.pallas_call(functools.partial(kernel, ctx_size, exp_size), out_shape=(...  103 us
    unnamed x4, local copies, waits for them, and re-layouts  6.09 us

profile of v1, /device:TPU:24, one launch (start us, length us, event | category | flops | bytes accessed | tf_op | source)
XLA Modules:
  0.0 110.1 jit_solution(18002131119247943845)
XLA Ops:
  0.6 1.4 %copy.14.step_ref = f32[128,16]{1,0:T(8,128)} copy(f32[128,16]{0,1:T(8,128)} %param.18) | data formatting | bytes 16384 | tf_op args[6]
  2.1 1.4 %copy.15.decay_ref = f32[128,16]{1,0:T(8,128)} copy(f32[128,16]{0,1:T(8,128)} %param.19) | data formatting | bytes 16384 | tf_op args[7]
  3.5 103.3 %shard_map.131 = (bf16[128,512]{1,0:T(8,128)(2,1)}, bf16[128,1024]{1,0:T(8,128)(2,1)}) custom-call(bf16[128,512]{1,0:T(8,128)(2,1)} %q_ref.1, bf16[128,128]{1,0:T(8,128)(2,1)} %k_ref.1, bf16[128,1024]{1,0:T(8,128)(2,1)} %x_ref.1, bf16[128,1024]{1,0:T(8,128)(2,1)} %gate_ref.1, bf16[128,128]{1,0:T(8,128)(2,1)} %write_ref.1, bf16[128,128]{1,0:T(8,128)(2,1)} %read_ref.1, ...), custom_call_target="tpu_custom_call" | custom-call | tf_op jit(solution)/shard_map/pallas_call | solution.py:518
  106.8 1.6 %copy.18 = bf16[128,512]{1,0:T(8,128)(2,1)} copy(bf16[128,512]{1,0:T(8,128)(2,1)} %get-tuple-element.4) | data formatting | bytes 262144
  108.4 1.7 %copy.19 = bf16[128,1024]{1,0:T(8,128)(2,1)} copy(bf16[128,1024]{1,0:T(8,128)(2,1)} %get-tuple-element.5) | data formatting | bytes 524288

commit v2 on v1

--- a/solution.py
+++ b/solution.py
@@ -33,20 +33,30 @@
 def kernel(
     ctx_size,
     exp_size,
-    q_ref,
-    k_ref,
-    x_ref,
-    gate_ref,
-    write_ref,
-    read_ref,
-    step_ref,
-    decay_ref,
-    skip_ref,
-    gain_ref,
-    freq_ref,
-    weight_ref,
+    *refs,
+):
+    inputs, refs = refs[:INPUTS], refs[INPUTS:]
+    attn_out, mixer_out = refs[:2]
+    staged, refs = refs[2 : 2 + INPUTS], refs[2 + INPUTS :]
+    (
+        k_ref,
+        decay_ref,
+        step_ref,
+        freq_ref,
+        x_ref,
+        write_ref,
+        read_ref,
+        q_ref,
+        skip_ref,
+        gate_ref,
+        gain_ref,
+        weight_ref,
+    ) = staged
+    (
     attn_ref,
     mixer_ref,
+    load_sem,
+    store_sem,
     local_state,
     state_in,
     state_out,
@@ -77,10 +87,10 @@
     ring_send,
     key_recv,
     value_recv,
-):
+    ) = refs
     z_size = ctx_size // ROWS_Y
     half = z_size // 2
-    heads = step_ref.shape[1]
+    heads = step_ref.shape[0]
     pairs = heads // 2
     groups = q_ref.shape[1] // HEAD_DIM
     state_rows = heads * MIXER_CHANNELS // ctx_size
@@ -91,13 +101,19 @@
 
     barrier = pltpu.get_barrier_semaphore()
 
+    def peer_of(i):
+        part, turn_y = lax.div(i, ROWS_Y), lax.rem(lax.rem(i, ROWS_Y) + 1, ROWS_Y)
+        odd = lax.rem(part, 2)
+        shift = half + (1 - 2 * odd) * lax.div(part + 1, 2)
+        return lax.rem(my_y + turn_y, ROWS_Y) * z_size + lax.rem(my_z + shift, z_size)
+
     def greet_ctx(i, c):
         pl.semaphore_signal(
-            barrier, inc=1, device_id={"ctx": lax.rem(me + i, ctx_size)}, device_id_type=MESH
+            barrier, inc=1, device_id={"ctx": peer_of(i)}, device_id_type=MESH
         )
         return c
 
-    lax.fori_loop(1, ctx_size, greet_ctx, 0)
+    lax.fori_loop(0, ctx_size - 1, greet_ctx, 0, unroll=UNROLL)
 
     def greet_exp(i, c):
         pl.semaphore_signal(
@@ -106,6 +122,15 @@
         return c
 
     lax.fori_loop(1, exp_size, greet_exp, 0)
+    loads = [
+        pltpu.make_async_copy(a, b, load_sem.at[i]) for i, (a, b) in enumerate(zip(inputs, staged))
+    ]
+    for load in loads:
+        load.start()
+    pad_a[...] = jnp.zeros_like(pad_a)
+    pad_b[...] = jnp.zeros_like(pad_b)
+    for load in loads[:4]:
+        load.wait()
 
     row = lax.broadcasted_iota(jnp.int32, (TOKENS, LANES), 0)
     lane = lax.broadcasted_iota(jnp.int32, (TOKENS, LANES), 1)
@@ -127,13 +152,17 @@
 
     key_all[me] = turn(k_ref[...])
 
-    tri = jnp.where(causal, 1.0, 0.0).astype(F32)
-    cumul = dot(tri, decay_ref[...], precision=HIGHEST)
+    tri = jnp.where(row <= lane, 1.0, 0.0).astype(F32)
+    cumul_t = dot(decay_ref[...], tri, precision=HIGHEST)
+    pad_a[0:heads, :] = cumul_t
+    pad_b[0:heads, :] = step_ref[...]
+    cumul = jnp.transpose(pad_a[...])
     ending = cumul[TOKENS - 1 : TOKENS, :]
-    ends_own[...] = jnp.zeros_like(ends_own)
-    ends_own[0, :, 0:heads] = ending
-    ends_all[me] = ends_own[0]
-    carry_weight = step_ref[...] * jnp.exp(ending - cumul)
+    ends_own[0] = ending
+    ends_all[me] = ending
+    carry_weight = jnp.transpose(pad_b[...]) * jnp.exp(ending - cumul)
+    for load in loads[4:6]:
+        load.wait()
     for j in range(pairs):
         weighted = x_ref[:, j * LANES : (j + 1) * LANES].astype(F32) * spread(carry_weight, j)
         turned = jnp.transpose(weighted).astype(BF16)
@@ -144,37 +173,36 @@
 
     pl.semaphore_wait(barrier, ctx_size + exp_size - 2)
 
-    def exchange(source, target, by_peer):
+    def exchange(*moves):
         def one(i, c):
-            part, turn_y = lax.div(i, ROWS_Y), lax.rem(lax.rem(i, ROWS_Y) + 1, ROWS_Y)
-            odd = lax.rem(part, 2)
-            shift = half + (1 - 2 * odd) * lax.div(part + 1, 2)
-            peer = lax.rem(my_y + turn_y, ROWS_Y) * z_size + lax.rem(my_z + shift, z_size)
-            pltpu.make_async_remote_copy(
-                src_ref=source.at[peer if by_peer else 0],
-                dst_ref=target.at[me],
-                send_sem=a2a_send.at[sem_at[0]],
-                recv_sem=a2a_recv.at[sem_at[0]],
-                device_id={"ctx": peer},
-                device_id_type=MESH,
-            ).start()
+            peer = peer_of(i)
+            for slot, source, target in moves:
+                pltpu.make_async_remote_copy(
+                    src_ref=source.at[peer if slot else 0],
+                    dst_ref=target.at[me],
+                    send_sem=a2a_send.at[slot],
+                    recv_sem=a2a_recv.at[slot],
+                    device_id={"ctx": peer},
+                    device_id_type=MESH,
+                ).start()
             return c
 
-        lax.fori_loop(0, ctx_size - 1, one, 0)
-
-    def exchange_wait(target):
+        lax.fori_loop(0, ctx_size - 1, one, 0, unroll=UNROLL)
+
+    def exchange_wait(slot, target):
         whole = target.at[pl.ds(0, ctx_size - 1)]
         done = pltpu.make_async_remote_copy(
             src_ref=whole,
             dst_ref=whole,
-            send_sem=a2a_send.at[sem_at[0]],
-            recv_sem=a2a_recv.at[sem_at[0]],
+            send_sem=a2a_send.at[slot],
+            recv_sem=a2a_recv.at[slot],
             device_id={"ctx": me},
             device_id_type=MESH,
         )
         done.wait_send()
         done.wait_recv()
 
+    key_length, value_length = half // SEGMENTS[0], half // SEGMENTS[1]
     block_b = jnp.where(my_y == 3, 1, 0)
     up_row = jnp.where(my_y == 1, 2, 3)
     right = my_y * z_size + lax.rem(my_z + 1, z_size)
@@ -200,11 +228,16 @@
             device_id_type=MESH,
         ).wait_recv()
 
-    def ring_open(buffer, recv, sem):
-        push(buffer, recv, me, right, sem)
-        if half > 1:
-            push(buffer, recv, me, left, sem)
-
+    def at_distance(d):
+        return lax.rem(my_z + d + 2 * z_size, z_size)
+
+    def launch(buffer, recv, sem, length, index):
+        for d in reversed(range(1, half + 1, length)):
+            push(buffer, recv, index, my_y * z_size + at_distance(d), sem)
+            if d < half:
+                push(buffer, recv, index, my_y * z_size + at_distance(-d), sem)
+
+    def ring_open(buffer, recv, sem, length):
         @pl.when(my_y == 0)
         def _():
             push(buffer, recv, me, z_size + my_z, sem)
@@ -214,75 +247,57 @@
         def _():
             push(buffer, recv, me, 3 * z_size + my_z, sem)
 
+        launch(buffer, recv, sem, length, me)
+
         @pl.when(my_y < 3)
         def _():
             push(buffer, recv, me, up_row * z_size + my_z, sem)
 
-    def ring_steps(low, high, buffer, recv, sem, compute):
+    def ring_steps(low, high, buffer, recv, sem, length, compute):
+        segments = half // length
+
         def step(s, c):
-            @pl.when((s >= 1) & (s <= half))
-            def _():
-                at = lax.rem(my_z - s + z_size, z_size)
-                own = my_y * z_size + at
-                arrived(buffer, recv, own, sem)
-
-                @pl.when(s < half)
-                def _():
-                    push(buffer, recv, own, right, sem)
-
-                @pl.when(my_y < 3)
-                def _():
-                    push(buffer, recv, own, up_row * z_size + my_z, sem)
-
-            @pl.when((s >= 1) & (s < half))
-            def _():
-                at = lax.rem(my_z + s, z_size)
-                own = my_y * z_size + at
-                arrived(buffer, recv, own, sem)
-
-                @pl.when(s < half - 1)
-                def _():
-                    push(buffer, recv, own, left, sem)
-
-                @pl.when(my_y < 3)
-                def _():
-                    push(buffer, recv, own, up_row * z_size + my_z, sem)
-
-            @pl.when((my_y > 0) & (s <= half))
-            def _():
-                at = lax.rem(my_z - s + z_size, z_size)
-                other = block_b * z_size + at
-                arrived(buffer, recv, other, sem)
-
-                @pl.when(s < half)
-                def _():
-                    push(buffer, recv, other, right, sem)
-
-                if half > 1:
-
-                    @pl.when(s == 0)
+            moving = (s >= 1) & (s <= length)
+
+            for source, lifted in ((my_y, True), (block_b, False)):
+                ready = moving if lifted else moving & (my_y > 0)
+                if not lifted:
+
+                    @pl.when((s == 0) & (my_y > 0))
                     def _():
-                        push(buffer, recv, other, left, sem)
-
-            @pl.when((my_y > 0) & (s >= 1) & (s < half))
-            def _():
-                at = lax.rem(my_z + s, z_size)
-                other = block_b * z_size + at
-                arrived(buffer, recv, other, sem)
-
-                @pl.when(s < half - 1)
-                def _():
-                    push(buffer, recv, other, left, sem)
+                        index = block_b * z_size + my_z
+                        arrived(buffer, recv, index, sem)
+                        launch(buffer, recv, sem, length, index)
+
+                for segment in range(segments):
+                    for side in range(2):
+                        d = s + segment * length
+
+                        @pl.when(ready & (d <= half - side))
+                        def _():
+                            index = source * z_size + at_distance(d if side else -d)
+                            arrived(buffer, recv, index, sem)
+
+                            @pl.when((s < length) & (d < half - side))
+                            def _():
+                                push(buffer, recv, index, left if side else right, sem)
+
+                            if lifted:
+
+                                @pl.when(my_y < 3)
+                                def _():
+                                    push(buffer, recv, index, up_row * z_size + my_z, sem)
 
             def visit(j, c):
-                side, row_y = lax.div(j, ROWS_Y), lax.rem(j, ROWS_Y)
+                segment, rest = lax.div(j, 2 * ROWS_Y), lax.rem(j, 2 * ROWS_Y)
+                side, row_y = lax.div(rest, ROWS_Y), lax.rem(rest, ROWS_Y)
                 relayed = (row_y != my_y) & (row_y != block_b) & (row_y < my_y)
                 back = s - jnp.where(relayed, 1, 0)
-                span = jnp.where(side == 0, back, z_size - back)
-                index = row_y * z_size + lax.rem(my_z - span + 2 * z_size, z_size)
-                low_ok = back >= side
-                high_ok = back <= half - side
-                valid = low_ok & high_ok & (row_y <= my_y)
+                d = back + segment * length
+                index = row_y * z_size + at_distance(jnp.where(side == 0, -d, d))
+                fits = (back <= length) & (d <= half - side)
+                starts = (back >= 1) | ((back == 0) & (segment == 0) & (side == 0))
+                valid = fits & starts & (row_y <= my_y)
 
                 @pl.when(valid & relayed)
                 def _():
@@ -294,12 +309,10 @@
 
                 return c
 
-            lax.fori_loop(0, 2 * ROWS_Y, visit, 0)
+            lax.fori_loop(0, segments * 2 * ROWS_Y, visit, 0)
             return c
 
         lax.fori_loop(low, high, step, 0)
-
-    ring_total = half + 2
 
     def ring_close(buffer, sem):
         ring = z_size - 1
@@ -319,35 +332,28 @@
                         device_id_type=MESH,
                     ).wait_send()
 
-    sem_at = [0]
-    ring_open(key_all, key_recv, ring_send.at[0])
-    exchange(ends_own, ends_all, False)
-    sem_at[0] = 1
-    exchange(local_state, state_in, True)
+    ring_open(key_all, key_recv, ring_send.at[0], key_length)
+    exchange((1, local_state, state_in), (0, ends_own, ends_all))
+    for load in loads[6:]:
+        load.wait()
 
     for g in range(groups):
         turned_q[g] = turn(q_ref[:, g * HEAD_DIM : (g + 1) * HEAD_DIM])
 
-    def score(g, index):
-        return dot(turned_q[g], key_all[index], ((1,), (1,)))
-
+    def score(index):
+        return dot(turned_q[...].reshape(groups * TOKENS, LANES), key_all[index], ((1,), (1,)))
+
+    own_score = score(me)
     for g in range(groups):
-        own_score = jnp.where(causal, score(g, me), LOWEST)
-        score_ref[me, g] = own_score
-        top_ref[g] = own_score
+        masked = jnp.where(causal, own_score[g * TOKENS : (g + 1) * TOKENS], LOWEST)
+        score_ref[me, g] = masked
+        top_ref[g] = masked
 
     def key_block(index):
-        for g in range(groups):
-            s = score(g, index)
-            score_ref[index, g] = s
-            top_ref[g] = jnp.maximum(top_ref[g], s)
-
-    pad_a[...] = jnp.zeros_like(pad_a)
-    pad_b[...] = jnp.zeros_like(pad_b)
-    pad_a[:, 0:heads] = cumul
-    pad_b[:, 0:heads] = step_ref[...]
-    cumul_t = jnp.transpose(pad_a[...])
-    step_t = jnp.transpose(pad_b[...])
+        s = score(index).reshape(groups, TOKENS, LANES)
+        score_ref[index] = s
+        top_ref[...] = jnp.maximum(top_ref[...], s)
+
     gram = dot(read_ref[...], write_ref[...], ((1,), (1,)))
     for j in range(pairs):
         x_pair = x_ref[:, j * LANES : (j + 1) * LANES]
@@ -355,7 +361,7 @@
         for part in range(2):
             h = 2 * j + part
             exponent = jnp.where(causal, cumul[:, h : h + 1] - cumul_t[h : h + 1, :], LOWEST)
-            mixing = (jnp.exp(exponent) * gram * step_t[h : h + 1, :]).astype(BF16)
+            mixing = (jnp.exp(exponent) * gram * step_ref[h : h + 1, :]).astype(BF16)
             keep = first if part == 0 else jnp.logical_not(first)
             term = dot(mixing, jnp.where(keep, x_pair, jnp.zeros_like(x_pair)))
             total = term if total is None else total + term
@@ -364,18 +370,16 @@
         )
         gated_ref[:, j * LANES : (j + 1) * LANES] = total + skip * x_pair.astype(F32)
 
-    split_a, split_b = min(SPLIT[0], ring_total), min(SPLIT[1], ring_total)
-    ring_steps(0, split_a, key_all, key_recv, ring_send.at[0], key_block)
-
-    sem_at[0] = 0
-    exchange_wait(ends_all)
+    split_a, split_b = min(SPLIT[0], key_length + 2), min(SPLIT[1], key_length + 2)
+    ring_steps(0, split_a, key_all, key_recv, ring_send.at[0], key_length, key_block)
+
+    exchange_wait(0, ends_all)
     head = lax.div(me * state_rows, MIXER_CHANNELS)
     chosen = jnp.where(row == head, 1.0, 0.0).astype(F32)
     decay_rows[...] = jnp.exp(
         dot(ends_all[...].reshape(ctx_size, LANES), chosen, precision=HIGHEST)
     )
-    sem_at[0] = 1
-    exchange_wait(state_in)
+    exchange_wait(1, state_in)
 
     def scan(b, state):
         state_out[b] = state.astype(BF16)
@@ -383,12 +387,11 @@
 
     lax.fori_loop(0, ctx_size, scan, jnp.zeros((state_rows, LANES), F32), unroll=8)
     state_back[me] = state_out[me]
-    sem_at[0] = 2
-    exchange(state_out, state_back, True)
-
-    ring_steps(split_a, split_b, key_all, key_recv, ring_send.at[0], key_block)
-
-    exchange_wait(state_back)
+    exchange((2, state_out, state_back))
+
+    ring_steps(split_a, split_b, key_all, key_recv, ring_send.at[0], key_length, key_block)
+
+    exchange_wait(2, state_back)
     growth = jnp.exp(cumul)
     squares = jnp.zeros((TOKENS, LANES), F32)
     per = LANES // state_rows
@@ -432,7 +435,7 @@
 
     lax.fori_loop(1, exp_size, scatter, 0)
 
-    ring_steps(split_b, ring_total, key_all, key_recv, ring_send.at[0], key_block)
+    ring_steps(split_b, key_length + 2, key_all, key_recv, ring_send.at[0], key_length, key_block)
     ring_close(key_all, ring_send.at[0])
 
     for g in range(groups):
@@ -470,25 +473,46 @@
     for e in range(1, exp_size):
         value = value + terms_in[e].astype(F32)
     value_all[me] = (value * factor).astype(BF16)
-    ring_open(value_all, value_recv, ring_send.at[1])
+    ring_open(value_all, value_recv, ring_send.at[1], value_length)
 
     for j in range(pairs):
         at = slice(j * LANES, (j + 1) * LANES)
         mixer_ref[:, at] = (gated_ref[:, at] * factor).astype(BF16)
 
+    store_mixer = pltpu.make_async_copy(mixer_ref, mixer_out, store_sem.at[0])
+    store_mixer.start()
+
     def value_block(index):
-        for g in range(groups):
-            out_ref[g] += dot(prob_ref[index, g], value_all[index])
+        probs = prob_ref[index].reshape(groups * TOKENS, LANES)
+        out_ref[...] += dot(probs, value_all[index]).reshape(groups, TOKENS, LANES)
 
     value_block(me)
-    ring_steps(0, ring_total, value_all, value_recv, ring_send.at[1], value_block)
+    ring_steps(
+        0, value_length + 2, value_all, value_recv, ring_send.at[1], value_length, value_block
+    )
     for g in range(groups):
         total = jnp.sum(sum_ref[g], axis=1, keepdims=True)
         attn_ref[:, g * HEAD_DIM : (g + 1) * HEAD_DIM] = (out_ref[g] / total).astype(BF16)
+    store_attn = pltpu.make_async_copy(attn_ref, attn_out, store_sem.at[1])
+    store_attn.start()
     ring_close(value_all, ring_send.at[1])
-
-
-SPLIT = (4, 8)
+    store_mixer.wait()
+    store_attn.wait()
+
+
+def hand_over(attn_in, mixer_in, attn_out, mixer_out, sem):
+    first = pltpu.make_async_copy(attn_in, attn_out, sem.at[0])
+    second = pltpu.make_async_copy(mixer_in, mixer_out, sem.at[1])
+    first.start()
+    second.start()
+    first.wait()
+    second.wait()
+
+
+SPLIT = (2, 6)
+SEGMENTS = (1, 2)
+INPUTS = 12
+UNROLL = 7
 
 
 def solution(mesh):
@@ -513,17 +537,38 @@
         state_rows = channels // ctx_size
         frequency = ROPE_BASE ** (-(2.0 * np.arange(HEAD_DIM // 2)) / HEAD_DIM)
         frequency = jnp.asarray(np.tile(frequency, 2)[None, :], F32)
-        vmem = functools.partial(pl.BlockSpec, memory_space=pltpu.VMEM)
         tile = (TOKENS, LANES)
-        return pl.pallas_call(
+        anywhere = pl.BlockSpec(memory_space=pl.ANY)
+        operands = (
+            key_rows,
+            log_decay.T,
+            step_size.T,
+            frequency,
+            mixer_input,
+            write_proj,
+            read_proj,
+            queries,
+            skip_gain.reshape(1, heads),
+            gate_input,
+            norm_gain.reshape(1, channels),
+            value_weight,
+        )
+        results = (
+            jax.ShapeDtypeStruct(queries.shape, BF16),
+            jax.ShapeDtypeStruct(mixer_input.shape, BF16),
+        )
+        staged = [pltpu.VMEM(a.shape, a.dtype) for a in operands]
+        held = [pltpu.VMEM(a.shape, a.dtype) for a in results]
+        found = pl.pallas_call(
             functools.partial(kernel, ctx_size, exp_size),
-            out_shape=(
-                jax.ShapeDtypeStruct(queries.shape, BF16),
-                jax.ShapeDtypeStruct(mixer_input.shape, BF16),
-            ),
-            in_specs=[vmem()] * 12,
-            out_specs=(vmem(), vmem()),
-            scratch_shapes=[
+            out_shape=results,
+            in_specs=[anywhere] * INPUTS,
+            out_specs=(anywhere, anywhere),
+            scratch_shapes=staged
+            + held
+            + [
+                pltpu.SemaphoreType.DMA((INPUTS,)),
+                pltpu.SemaphoreType.DMA((2,)),
                 pltpu.VMEM((ctx_size, state_rows, LANES), BF16),
                 pltpu.VMEM((ctx_size, state_rows, LANES), BF16),
                 pltpu.VMEM((ctx_size, state_rows, LANES), BF16),
@@ -558,20 +603,15 @@
             compiler_params=pltpu.CompilerParams(
                 collective_id=0, has_side_effects=True, vmem_limit_bytes=56 * 1024 * 1024
             ),
-        )(
-            queries,
-            key_rows,
-            mixer_input,
-            gate_input,
-            write_proj,
-            read_proj,
-            step_size,
-            log_decay,
-            skip_gain.reshape(1, heads),
-            norm_gain.reshape(1, channels),
-            frequency,
-            value_weight,
-        )
+        )(*operands)
+        return pl.pallas_call(
+            hand_over,
+            out_shape=results,
+            in_specs=[pl.BlockSpec(memory_space=pltpu.VMEM)] * 2,
+            out_specs=(anywhere, anywhere),
+            scratch_shapes=[pltpu.SemaphoreType.DMA((2,))],
+            compiler_params=pltpu.CompilerParams(vmem_limit_bytes=2 * 1024 * 1024),
+        )(*found)
 
     return jax.shard_map(
         on_device,

time: 110 us -> 100 us (0.909)
  Pallas kernels: 103 us -> 97.7 us
  local copies, waits for them, and re-layouts: 6.09 us -> 1.85 us
    pallas_call x1 -> x2, Pallas kernels: 103 us -> 97.7 us  [the longest x1 96.9 us: on_device(): pl.pallas_call(functools.partial(kernel, ctx_size, exp_size), out_shape=r...]
    unnamed x4, local copies, waits for them, and re-layouts: 6.09 us -> 1.85 us
where the time goes in v2:
time: 100 us
  Pallas kernels  97.7 us (98%)
  local copies, waits for them, and re-layouts  1.85 us (2%)
    pallas_call x1, Pallas kernels, on_device(): pl.pallas_call(functools.partial(kernel, ctx_size, exp_size), out_shape=r...  96.9 us

profile of v2, /device:TPU:24, one launch (start us, length us, event | category | flops | bytes accessed | tf_op | source)
XLA Modules:
  0.0 100.2 jit_solution(11289155055793155313)
XLA Ops:
  0.6 96.9 %shard_map.131 = (bf16[128,512]{1,0:T(8,128)(2,1)}, bf16[128,1024]{1,0:T(8,128)(2,1)}) custom-call(bf16[128,128]{1,0:T(8,128)(2,1)} %refs_0_.1, f32[16,128]{1,0:T(8,128)} %bitcast.4, f32[16,128]{1,0:T(8,128)} %bitcast.5, f32[1,128]{1,0:T(1,128)} %constant.2.clone.refs_3_, bf16[128,1024]{1,0:T(8,128)(2,1)} %refs_4_.1, bf16[128,128]{1,0:T(8,128)(2,1)} %refs_5_.1, ...), custom_call_target="tpu_custom_call" | custom-call | tf_op jit(solution)/shard_map/pallas_call | solution.py:562
  97.6 0.0 copy-start
  97.6 0.9 copy-done
  98.5 0.0 copy-start.1
  98.5 0.9 copy-done.1
  99.4 0.8 shard_map.132
Async XLA Ops:
  97.6 1.0 copy-start
  98.5 0.9 copy-start.1

commit v3 on v2

--- a/solution.py
+++ b/solution.py
@@ -36,7 +36,7 @@
     *refs,
 ):
     inputs, refs = refs[:INPUTS], refs[INPUTS:]
-    attn_out, mixer_out = refs[:2]
+    attn_ref, mixer_ref = refs[:2]
     staged, refs = refs[2 : 2 + INPUTS], refs[2 + INPUTS :]
     (
         k_ref,
@@ -53,10 +53,7 @@
         weight_ref,
     ) = staged
     (
-    attn_ref,
-    mixer_ref,
     load_sem,
-    store_sem,
     local_state,
     state_in,
     state_out,
@@ -208,91 +205,118 @@
     right = my_y * z_size + lax.rem(my_z + 1, z_size)
     left = my_y * z_size + lax.rem(my_z + z_size - 1, z_size)
 
-    def push(buffer, recv, index, peer, sem):
-        pltpu.make_async_remote_copy(
-            src_ref=buffer.at[index],
-            dst_ref=buffer.at[index],
-            send_sem=sem,
-            recv_sem=recv.at[index],
-            device_id={"ctx": peer},
-            device_id_type=MESH,
-        ).start()
-
-    def arrived(buffer, recv, index, sem):
-        pltpu.make_async_remote_copy(
-            src_ref=buffer.at[index],
-            dst_ref=buffer.at[index],
-            send_sem=sem,
-            recv_sem=recv.at[index],
-            device_id={"ctx": me},
-            device_id_type=MESH,
-        ).wait_recv()
+    def piece(buffer, recv, index, part):
+        pieces = recv.shape[1]
+        size = TOKENS // pieces
+        at = index if pieces == 1 else (index, pl.ds(part * size, size))
+        return buffer.at[at], recv.at[index, part]
+
+    def push(buffer, recv, index, peer, sem, part=None):
+        for p in range(recv.shape[1]) if part is None else (part,):
+            block, landed = piece(buffer, recv, index, p)
+            pltpu.make_async_remote_copy(
+                src_ref=block,
+                dst_ref=block,
+                send_sem=sem,
+                recv_sem=landed,
+                device_id={"ctx": peer},
+                device_id_type=MESH,
+            ).start()
+
+    def arrived(buffer, recv, index, sem, part=None):
+        for p in range(recv.shape[1]) if part is None else (part,):
+            block, landed = piece(buffer, recv, index, p)
+            pltpu.make_async_remote_copy(
+                src_ref=block,
+                dst_ref=block,
+                send_sem=sem,
+                recv_sem=landed,
+                device_id={"ctx": me},
+                device_id_type=MESH,
+            ).wait_recv()
 
     def at_distance(d):
         return lax.rem(my_z + d + 2 * z_size, z_size)
 
-    def launch(buffer, recv, sem, length, index):
+    def launch(buffer, recv, sem, length, row_y):
         for d in reversed(range(1, half + 1, length)):
-            push(buffer, recv, index, my_y * z_size + at_distance(d), sem)
+            push(buffer, recv, me, row_y * z_size + at_distance(d), sem)
             if d < half:
-                push(buffer, recv, index, my_y * z_size + at_distance(-d), sem)
-
-    def ring_open(buffer, recv, sem, length):
+                push(buffer, recv, me, row_y * z_size + at_distance(-d), sem)
+
+    def lift(buffer, recv, index, sem, by_y, part=None):
+        @pl.when(my_y < 3)
+        def _():
+            push(buffer, recv, index, up_row * z_size + my_z, sem, part)
+
+        if by_y:
+
+            @pl.when(my_y == 0)
+            def _():
+                push(buffer, recv, index, z_size + my_z, sem, part)
+
+    def ring_open(buffer, recv, sem, length, by_y):
+        launch(buffer, recv, sem, length, my_y)
+        lift(buffer, recv, me, sem, by_y)
+        if by_y:
+            return
+
+        @pl.when(my_y == 1)
+        def _():
+            launch(buffer, recv, sem, length, 3)
+            push(buffer, recv, me, 3 * z_size + my_z, sem)
+
         @pl.when(my_y == 0)
         def _():
+            launch(buffer, recv, sem, length, 2)
+            launch(buffer, recv, sem, length, 1)
+            push(buffer, recv, me, 2 * z_size + my_z, sem)
             push(buffer, recv, me, z_size + my_z, sem)
-            push(buffer, recv, me, 2 * z_size + my_z, sem)
-
-        @pl.when(my_y == 1)
-        def _():
-            push(buffer, recv, me, 3 * z_size + my_z, sem)
-
-        launch(buffer, recv, sem, length, me)
-
-        @pl.when(my_y < 3)
-        def _():
-            push(buffer, recv, me, up_row * z_size + my_z, sem)
-
-    def ring_steps(low, high, buffer, recv, sem, length, compute):
+
+    def ring_steps(low, high, buffer, recv, sem, length, by_y, compute):
         segments = half // length
 
         def step(s, c):
-            moving = (s >= 1) & (s <= length)
-
-            for source, lifted in ((my_y, True), (block_b, False)):
-                ready = moving if lifted else moving & (my_y > 0)
+            for source, lifted in ((my_y, True),) if by_y else ((my_y, True), (block_b, False)):
                 if not lifted:
 
                     @pl.when((s == 0) & (my_y > 0))
                     def _():
                         index = block_b * z_size + my_z
                         arrived(buffer, recv, index, sem)
-                        launch(buffer, recv, sem, length, index)
 
                 for segment in range(segments):
                     for side in range(2):
-                        d = s + segment * length
-
-                        @pl.when(ready & (d <= half - side))
+                        hop = s - segment
+                        d = hop + segment * length
+                        ready = (hop >= 1) & (hop <= length) & (d <= half - side)
+                        if not lifted:
+                            ready = ready & (my_y > 0)
+
+                        @pl.when(ready)
                         def _():
                             index = source * z_size + at_distance(d if side else -d)
-                            arrived(buffer, recv, index, sem)
-
-                            @pl.when((s < length) & (d < half - side))
-                            def _():
-                                push(buffer, recv, index, left if side else right, sem)
-
-                            if lifted:
-
-                                @pl.when(my_y < 3)
+                            for part in range(recv.shape[1]):
+                                arrived(buffer, recv, index, sem, part)
+
+                                @pl.when((hop < length) & (d < half - side))
                                 def _():
-                                    push(buffer, recv, index, up_row * z_size + my_z, sem)
+                                    push(buffer, recv, index, left if side else right, sem, part)
+
+                                if lifted:
+                                    lift(buffer, recv, index, sem, by_y, part)
 
             def visit(j, c):
                 segment, rest = lax.div(j, 2 * ROWS_Y), lax.rem(j, 2 * ROWS_Y)
                 side, row_y = lax.div(rest, ROWS_Y), lax.rem(rest, ROWS_Y)
-                relayed = (row_y != my_y) & (row_y != block_b) & (row_y < my_y)
-                back = s - jnp.where(relayed, 1, 0)
+                if by_y:
+                    relayed = row_y < my_y
+                    twice = ((my_y == 2) & (row_y == 0)) | ((my_y == 3) & (row_y == 1))
+                    lag = jnp.where(relayed, jnp.where(twice, 2, 1), 0)
+                else:
+                    relayed = (row_y != my_y) & (row_y != block_b) & (row_y < my_y)
+                    lag = jnp.where(relayed, 1, 0)
+                back = s - segment - lag
                 d = back + segment * length
                 index = row_y * z_size + at_distance(jnp.where(side == 0, -d, d))
                 fits = (back <= length) & (d <= half - side)
@@ -303,6 +327,12 @@
                 def _():
                     arrived(buffer, recv, index, sem)
 
+                if by_y:
+
+                    @pl.when(valid & (my_y < 3) & (row_y + 1 == my_y))
+                    def _():
+                        push(buffer, recv, index, (my_y + 1) * z_size + my_z, sem)
+
                 @pl.when(valid & (index < me))
                 def _():
                     compute(index)
@@ -314,9 +344,22 @@
 
         lax.fori_loop(low, high, step, 0)
 
-    def ring_close(buffer, sem):
+    def ring_last(length, by_y):
+        return length + half // length + (2 if by_y else 1)
+
+    def ring_close(buffer, sem, length, by_y):
         ring = z_size - 1
-        for y, count in enumerate((ring + 2 + z_size, 2 * ring + 1 + z_size, 2 * ring + z_size, 2 * ring)):
+        opened = 2 * (half // length) - (1 if (half - 1) % length == 0 else 0)
+        relays = ring - opened
+        counts = (
+            ring + z_size + 2 * (opened + 1),
+            ring + z_size + opened + 1 + relays,
+            ring + z_size + relays,
+            ring + relays,
+        )
+        if by_y:
+            counts = (ring + 2 * z_size,) * 3 + (ring,)
+        for y, count in enumerate(counts):
 
             @pl.when(my_y == y)
             def _():
@@ -332,7 +375,7 @@
                         device_id_type=MESH,
                     ).wait_send()
 
-    ring_open(key_all, key_recv, ring_send.at[0], key_length)
+    ring_open(key_all, key_recv, ring_send.at[0], key_length, True)
     exchange((1, local_state, state_in), (0, ends_own, ends_all))
     for load in loads[6:]:
         load.wait()
@@ -370,8 +413,8 @@
         )
         gated_ref[:, j * LANES : (j + 1) * LANES] = total + skip * x_pair.astype(F32)
 
-    split_a, split_b = min(SPLIT[0], key_length + 2), min(SPLIT[1], key_length + 2)
-    ring_steps(0, split_a, key_all, key_recv, ring_send.at[0], key_length, key_block)
+    split_a, split_b = min(SPLIT[0], ring_last(key_length, True)), min(SPLIT[1], ring_last(key_length, True))
+    ring_steps(0, split_a, key_all, key_recv, ring_send.at[0], key_length, True, key_block)
 
     exchange_wait(0, ends_all)
     head = lax.div(me * state_rows, MIXER_CHANNELS)
@@ -389,7 +432,7 @@
     state_back[me] = state_out[me]
     exchange((2, state_out, state_back))
 
-    ring_steps(split_a, split_b, key_all, key_recv, ring_send.at[0], key_length, key_block)
+    ring_steps(split_a, split_b, key_all, key_recv, ring_send.at[0], key_length, True, key_block)
 
     exchange_wait(2, state_back)
     growth = jnp.exp(cumul)
@@ -407,14 +450,15 @@
         scaled_ref[:, at] = scaled.astype(BF16)
     ones = jnp.ones((8, LANES), F32)
     square_own[0] = dot(ones, squares, ((1,), (1,)), precision=HIGHEST)
-    for e in range(exp_size):
-        terms = dot(scaled_ref[...], weight_ref[:, e * LANES : (e + 1) * LANES])
-        terms_ref[e] = terms.astype(BF16)
-    terms_in[col] = terms_ref[col]
     square_in[col] = square_own[0]
 
+    def value_terms(e):
+        at = pl.ds(pl.multiple_of(e * LANES, LANES), LANES)
+        return dot(scaled_ref[...], weight_ref[:, at]).astype(BF16)
+
     def scatter(i, c):
-        peer = lax.rem(col + i, exp_size)
+        order = exp_size // 2 + (1 - 2 * lax.rem(i, 2)) * lax.div(i + 1, 2)
+        peer = lax.rem(col + order, exp_size)
         pltpu.make_async_remote_copy(
             src_ref=square_own.at[0],
             dst_ref=square_in.at[col],
@@ -423,6 +467,7 @@
             device_id={"exp": peer},
             device_id_type=MESH,
         ).start()
+        terms_ref[peer] = value_terms(peer)
         pltpu.make_async_remote_copy(
             src_ref=terms_ref.at[peer],
             dst_ref=terms_in.at[col],
@@ -433,10 +478,11 @@
         ).start()
         return c
 
-    lax.fori_loop(1, exp_size, scatter, 0)
-
-    ring_steps(split_b, key_length + 2, key_all, key_recv, ring_send.at[0], key_length, key_block)
-    ring_close(key_all, ring_send.at[0])
+    lax.fori_loop(0, exp_size - 1, scatter, 0)
+    terms_in[col] = value_terms(col)
+
+    ring_steps(split_b, ring_last(key_length, True), key_all, key_recv, ring_send.at[0], key_length, True, key_block)
+    ring_close(key_all, ring_send.at[0], key_length, True)
 
     for g in range(groups):
         top_ref[g] = jnp.broadcast_to(jnp.max(top_ref[g], axis=1, keepdims=True), (TOKENS, LANES))
@@ -473,31 +519,24 @@
     for e in range(1, exp_size):
         value = value + terms_in[e].astype(F32)
     value_all[me] = (value * factor).astype(BF16)
-    ring_open(value_all, value_recv, ring_send.at[1], value_length)
+    ring_open(value_all, value_recv, ring_send.at[1], value_length, False)
 
     for j in range(pairs):
         at = slice(j * LANES, (j + 1) * LANES)
         mixer_ref[:, at] = (gated_ref[:, at] * factor).astype(BF16)
 
-    store_mixer = pltpu.make_async_copy(mixer_ref, mixer_out, store_sem.at[0])
-    store_mixer.start()
-
     def value_block(index):
         probs = prob_ref[index].reshape(groups * TOKENS, LANES)
         out_ref[...] += dot(probs, value_all[index]).reshape(groups, TOKENS, LANES)
 
     value_block(me)
     ring_steps(
-        0, value_length + 2, value_all, value_recv, ring_send.at[1], value_length, value_block
+        0, ring_last(value_length, False), value_all, value_recv, ring_send.at[1], value_length, False, value_block
     )
     for g in range(groups):
         total = jnp.sum(sum_ref[g], axis=1, keepdims=True)
         attn_ref[:, g * HEAD_DIM : (g + 1) * HEAD_DIM] = (out_ref[g] / total).astype(BF16)
-    store_attn = pltpu.make_async_copy(attn_ref, attn_out, store_sem.at[1])
-    store_attn.start()
-    ring_close(value_all, ring_send.at[1])
-    store_mixer.wait()
-    store_attn.wait()
+    ring_close(value_all, ring_send.at[1], value_length, False)
 
 
 def hand_over(attn_in, mixer_in, attn_out, mixer_out, sem):
@@ -509,8 +548,9 @@
     second.wait()
 
 
-SPLIT = (2, 6)
+SPLIT = (3, 8)
 SEGMENTS = (1, 2)
+PIECES = (1, 1)
 INPUTS = 12
 UNROLL = 7
 
@@ -558,17 +598,14 @@
             jax.ShapeDtypeStruct(mixer_input.shape, BF16),
         )
         staged = [pltpu.VMEM(a.shape, a.dtype) for a in operands]
-        held = [pltpu.VMEM(a.shape, a.dtype) for a in results]
         found = pl.pallas_call(
             functools.partial(kernel, ctx_size, exp_size),
-            out_shape=results,
+            out_shape=tuple(pltpu.VMEM(a.shape, a.dtype) for a in results),
             in_specs=[anywhere] * INPUTS,
-            out_specs=(anywhere, anywhere),
+            out_specs=(pl.BlockSpec(memory_space=pltpu.VMEM),) * 2,
             scratch_shapes=staged
-            + held
             + [
                 pltpu.SemaphoreType.DMA((INPUTS,)),
-                pltpu.SemaphoreType.DMA((2,)),
                 pltpu.VMEM((ctx_size, state_rows, LANES), BF16),
                 pltpu.VMEM((ctx_size, state_rows, LANES), BF16),
                 pltpu.VMEM((ctx_size, state_rows, LANES), BF16),
@@ -597,8 +634,8 @@
                 pltpu.SemaphoreType.DMA((2,)),
                 pltpu.SemaphoreType.DMA((2,)),
                 pltpu.SemaphoreType.DMA((2,)),
-                pltpu.SemaphoreType.DMA((ctx_size,)),
-                pltpu.SemaphoreType.DMA((ctx_size,)),
+                pltpu.SemaphoreType.DMA((ctx_size, PIECES[0])),
+                pltpu.SemaphoreType.DMA((ctx_size, PIECES[1])),
             ],
             compiler_params=pltpu.CompilerParams(
                 collective_id=0, has_side_effects=True, vmem_limit_bytes=56 * 1024 * 1024

time: 100 us -> 96.4 us (0.964); the launches traced: 100 us -> 95.3 us
  Pallas kernels: 97.7 us -> 94.7 us
  local copies, waits for them, and re-layouts: 1.85 us -> 0 us
    pallas_call x1, Pallas kernels: 96.9 us -> 93.9 us  [on_device(): pl.pallas_call(functools.partial(kernel, ctx_size, exp_size), out_shape=t...]
    unnamed x4 -> x0, local copies, waits for them, and re-layouts: 1.85 us -> none
where the time goes in v3:
time: 96.4 us; the launch traced here: 95.3 us
  Pallas kernels  94.7 us (98%)
    pallas_call x1, Pallas kernels, on_device(): pl.pallas_call(functools.partial(kernel, ctx_size, exp_size), out_shape=t...  93.9 us

profile of v3, /device:TPU:24, one launch (start us, length us, event | category | flops | bytes accessed | tf_op | source)
XLA Modules:
  0.0 95.3 jit_solution(6522684755346364462)
XLA Ops:
  0.6 93.9 %shard_map.131 = (bf16[128,512]{1,0:T(8,128)(2,1)S(1)}, bf16[128,1024]{1,0:T(8,128)(2,1)S(1)}) custom-call(bf16[128,128]{1,0:T(8,128)(2,1)} %refs_0_.1, f32[16,128]{1,0:T(8,128)} %bitcast.4, f32[16,128]{1,0:T(8,128)} %bitcast.5, f32[1,128]{1,0:T(1,128)} %constant.2.clone.refs_3_, bf16[128,1024]{1,0:T(8,128)(2,1)} %refs_4_.1, bf16[128,128]{1,0:T(8,128)(2,1)} %refs_5_.1, ...), custom_call_target="tpu_custom_call" | custom-call | tf_op jit(solution)/shard_map/pallas_call | solution.py:601
  94.6 0.8 shard_map.132

commit v4 on v3

--- a/solution.py
+++ b/solution.py
@@ -110,7 +110,7 @@
         )
         return c
 
-    lax.fori_loop(0, ctx_size - 1, greet_ctx, 0, unroll=UNROLL)
+    lax.fori_loop(0, ctx_size - 1, greet_ctx, 0, unroll=7 if ctx_size == 64 else 1)
 
     def greet_exp(i, c):
         pl.semaphore_signal(
@@ -170,7 +170,7 @@
 
     pl.semaphore_wait(barrier, ctx_size + exp_size - 2)
 
-    def exchange(*moves):
+    def exchange(low, high, *moves):
         def one(i, c):
             peer = peer_of(i)
             for slot, source, target in moves:
@@ -184,9 +184,9 @@
                 ).start()
             return c
 
-        lax.fori_loop(0, ctx_size - 1, one, 0, unroll=UNROLL)
-
-    def exchange_wait(slot, target):
+        lax.fori_loop(low, high, one, 0, unroll=4 if (high - low) % 4 == 0 else 5 if (high - low) % 5 == 0 else 1)
+
+    def exchange_wait(slot, target, sent=False):
         whole = target.at[pl.ds(0, ctx_size - 1)]
         done = pltpu.make_async_remote_copy(
             src_ref=whole,
@@ -196,8 +196,7 @@
             device_id={"ctx": me},
             device_id_type=MESH,
         )
-        done.wait_send()
-        done.wait_recv()
+        done.wait_send() if sent else done.wait_recv()
 
     key_length, value_length = half // SEGMENTS[0], half // SEGMENTS[1]
     block_b = jnp.where(my_y == 3, 1, 0)
@@ -376,7 +375,9 @@
                     ).wait_send()
 
     ring_open(key_all, key_recv, ring_send.at[0], key_length, True)
-    exchange((1, local_state, state_in), (0, ends_own, ends_all))
+    cuts = [ctx_size * part // SHARES for part in range(SHARES)] + [ctx_size - 1]
+    outgoing = ((1, local_state, state_in), (0, ends_own, ends_all))
+    exchange(cuts[0], cuts[1], *outgoing)
     for load in loads[6:]:
         load.wait()
 
@@ -413,8 +414,21 @@
         )
         gated_ref[:, j * LANES : (j + 1) * LANES] = total + skip * x_pair.astype(F32)
 
-    split_a, split_b = min(SPLIT[0], ring_last(key_length, True)), min(SPLIT[1], ring_last(key_length, True))
-    ring_steps(0, split_a, key_all, key_recv, ring_send.at[0], key_length, True, key_block)
+    total_steps = ring_last(key_length, True)
+    done = [0]
+
+    def key_steps(upto):
+        upto = min(upto, total_steps)
+        if upto > done[0]:
+            ring_steps(
+                done[0], upto, key_all, key_recv, ring_send.at[0], key_length, True, key_block
+            )
+        done[0] = max(upto, done[0])
+
+    for part in range(1, SHARES):
+        key_steps(STEPS[0][part - 1])
+        exchange(cuts[part], cuts[part + 1], *outgoing)
+    key_steps(STEPS[0][SHARES - 1])
 
     exchange_wait(0, ends_all)
     head = lax.div(me * state_rows, MIXER_CHANNELS)
@@ -430,9 +444,10 @@
 
     lax.fori_loop(0, ctx_size, scan, jnp.zeros((state_rows, LANES), F32), unroll=8)
     state_back[me] = state_out[me]
-    exchange((2, state_out, state_back))
-
-    ring_steps(split_a, split_b, key_all, key_recv, ring_send.at[0], key_length, True, key_block)
+    for part in range(SHARES):
+        exchange(cuts[part], cuts[part + 1], (2, state_out, state_back))
+        key_steps(STEPS[1][part])
+
 
     exchange_wait(2, state_back)
     growth = jnp.exp(cumul)
@@ -481,8 +496,7 @@
     lax.fori_loop(0, exp_size - 1, scatter, 0)
     terms_in[col] = value_terms(col)
 
-    ring_steps(split_b, ring_last(key_length, True), key_all, key_recv, ring_send.at[0], key_length, True, key_block)
-    ring_close(key_all, ring_send.at[0], key_length, True)
+    key_steps(total_steps)
 
     for g in range(groups):
         top_ref[g] = jnp.broadcast_to(jnp.max(top_ref[g], axis=1, keepdims=True), (TOKENS, LANES))
@@ -498,7 +512,7 @@
 
     lax.fori_loop(0, me + 1, weigh, 0)
 
-    for slot, target in ((0, square_in), (1, terms_in)):
+    def scatter_wait(slot, target, sent=False):
         whole = target.at[pl.ds(0, exp_size - 1)]
         done = pltpu.make_async_remote_copy(
             src_ref=whole,
@@ -508,8 +522,10 @@
             device_id={"exp": col},
             device_id_type=MESH,
         )
-        done.wait_send()
-        done.wait_recv()
+        done.wait_send() if sent else done.wait_recv()
+
+    for slot, target in ((0, square_in), (1, terms_in)):
+        scatter_wait(slot, target)
     square_row = square_in[0]
     for e in range(1, exp_size):
         square_row = square_row + square_in[e]
@@ -536,7 +552,12 @@
     for g in range(groups):
         total = jnp.sum(sum_ref[g], axis=1, keepdims=True)
         attn_ref[:, g * HEAD_DIM : (g + 1) * HEAD_DIM] = (out_ref[g] / total).astype(BF16)
+    ring_close(key_all, ring_send.at[0], key_length, True)
     ring_close(value_all, ring_send.at[1], value_length, False)
+    for slot, target in ((0, ends_all), (1, state_in), (2, state_back)):
+        exchange_wait(slot, target, True)
+    for slot, target in ((0, square_in), (1, terms_in)):
+        scatter_wait(slot, target, True)
 
 
 def hand_over(attn_in, mixer_in, attn_out, mixer_out, sem):
@@ -548,11 +569,11 @@
     second.wait()
 
 
-SPLIT = (3, 8)
+SHARES = 2
+STEPS = ((2, 4), (6, 8))
 SEGMENTS = (1, 2)
 PIECES = (1, 1)
 INPUTS = 12
-UNROLL = 7
 
 
 def solution(mesh):

time: 96.4 us -> 94.1 us (0.976)
  Pallas kernels: 94.7 us -> 92.7 us
    pallas_call x1, Pallas kernels: 93.9 us -> 92 us  [on_device(): pl.pallas_call(functools.partial(kernel, ctx_size, exp_size), out_shape=t...]
where the time goes in v4:
time: 94.1 us; the launch traced here: 93.4 us
  Pallas kernels  92.7 us (99%)
    pallas_call x1, Pallas kernels, on_device(): pl.pallas_call(functools.partial(kernel, ctx_size, exp_size), out_shape=t...  92 us

profile of v4, /device:TPU:24, one launch (start us, length us, event | category | flops | bytes accessed | tf_op | source)
XLA Modules:
  0.0 93.4 jit_solution(8397798861137598287)
XLA Ops:
  0.6 92.0 %shard_map.131 = (bf16[128,512]{1,0:T(8,128)(2,1)S(1)}, bf16[128,1024]{1,0:T(8,128)(2,1)S(1)}) custom-call(bf16[128,128]{1,0:T(8,128)(2,1)} %refs_0_.1, f32[16,128]{1,0:T(8,128)} %bitcast.4, f32[16,128]{1,0:T(8,128)} %bitcast.5, f32[1,128]{1,0:T(1,128)} %constant.2.clone.refs_3_, bf16[128,1024]{1,0:T(8,128)(2,1)} %refs_4_.1, bf16[128,128]{1,0:T(8,128)(2,1)} %refs_5_.1, ...), custom_call_target="tpu_custom_call" | custom-call | tf_op jit(solution)/shard_map/pallas_call | solution.py:622
  92.6 0.8 shard_map.132

commit v5 on v4

--- a/solution.py
+++ b/solution.py
@@ -286,7 +286,7 @@
 
                 for segment in range(segments):
                     for side in range(2):
-                        hop = s - segment
+                        hop = s
                         d = hop + segment * length
                         ready = (hop >= 1) & (hop <= length) & (d <= half - side)
                         if not lifted:
@@ -315,7 +315,7 @@
                 else:
                     relayed = (row_y != my_y) & (row_y != block_b) & (row_y < my_y)
                     lag = jnp.where(relayed, 1, 0)
-                back = s - segment - lag
+                back = s - lag
                 d = back + segment * length
                 index = row_y * z_size + at_distance(jnp.where(side == 0, -d, d))
                 fits = (back <= length) & (d <= half - side)
@@ -344,7 +344,7 @@
         lax.fori_loop(low, high, step, 0)
 
     def ring_last(length, by_y):
-        return length + half // length + (2 if by_y else 1)
+        return length + (3 if by_y else 2)
 
     def ring_close(buffer, sem, length, by_y):
         ring = z_size - 1

time: 94.1 us -> 93.6 us (level); the launches traced: 93.4 us -> 91.7 us
  Pallas kernels: 92.7 us -> 91.1 us
    pallas_call x1, Pallas kernels: 92 us -> 90.3 us  [on_device(): pl.pallas_call(functools.partial(kernel, ctx_size, exp_size), out_shape=t...]
where the time goes in v5:
time: 93.6 us; the launch traced here: 91.7 us
  Pallas kernels  91.1 us (97%)
    pallas_call x1, Pallas kernels, on_device(): pl.pallas_call(functools.partial(kernel, ctx_size, exp_size), out_shape=t...  90.3 us

profile of v5, /device:TPU:24, one launch (start us, length us, event | category | flops | bytes accessed | tf_op | source)
XLA Modules:
  0.0 91.7 jit_solution(16655017866194306055)
XLA Ops:
  0.6 90.3 %shard_map.131 = (bf16[128,512]{1,0:T(8,128)(2,1)S(1)}, bf16[128,1024]{1,0:T(8,128)(2,1)S(1)}) custom-call(bf16[128,128]{1,0:T(8,128)(2,1)} %refs_0_.1, f32[16,128]{1,0:T(8,128)} %bitcast.4, f32[16,128]{1,0:T(8,128)} %bitcast.5, f32[1,128]{1,0:T(1,128)} %constant.2.clone.refs_3_, bf16[128,1024]{1,0:T(8,128)(2,1)} %refs_4_.1, bf16[128,128]{1,0:T(8,128)(2,1)} %refs_5_.1, ...), custom_call_target="tpu_custom_call" | custom-call | tf_op jit(solution)/shard_map/pallas_call | solution.py:622
  91.0 0.8 shard_map.132
